TPU v7x, 256 devices: a whole 4x4x8 slice. The times are simulated.
256 devices in a mesh: row: 32 (over z_lo, x, core), col: 8 (over z_hi, y).
Axes of the slice: x: 4, y: 4, z: 8 (z_hi: 2, z_lo: 4; z = z_hi * 4 + z_lo), core: 2. Of those that a mesh axis runs over, the one named last changes fastest.
Arguments:
- pair: bfloat16 [512, 512, 128], P('row', 'col'), may hold values from -6 to 6
- cotangent: bfloat16 [64, 512, 512], P(None, 'row', 'col'), may hold values from -0.59765625 to 0.59765625
- w_left: bfloat16 [128, 64], replicated, may hold values from -0.5 to 0.5
- w_left_gate: bfloat16 [128, 64], replicated, may hold values from -0.5 to 0.5
- w_right: bfloat16 [128, 64], replicated, may hold values from -0.5 to 0.5
- w_right_gate: bfloat16 [128, 64], replicated, may hold values from -0.5 to 0.5
Outputs:
- pair_gradient: bfloat16 [512, 512, 128], P('row', 'col')
- grad_left: float32 [128, 64], replicated
- grad_left_gate: float32 [128, 64], replicated
- grad_right: float32 [128, 64], replicated
- grad_right_gate: float32 [128, 64], replicated
All inputs are finite; a program needn't handle non-finite values.
Results may differ from a plain program's by a relative error of at most 0.0082.
Values may be sent and summed in bfloat16 or wider, within the bound.
A program may use at most 64 MiB of HBM per device.

v0:
```python
import jax
import jax.numpy as jnp
from jax import lax
from jax.sharding import PartitionSpec as P


def shards(pair, cotangent, w_left, w_left_gate, w_right, w_right_gate):
    pair_f = pair.astype(jnp.float32)
    average = jnp.mean(pair_f, axis=-1, keepdims=True)
    centered_input = pair_f - average
    variance = jnp.mean(centered_input * centered_input, axis=-1, keepdims=True)
    inverse_scale = 1.0 / jnp.sqrt(variance + 1e-05)
    standardized_input = centered_input * inverse_scale
    normalized_input = standardized_input.astype(jnp.bfloat16)
    stacked = jnp.concatenate([w_left, w_left_gate, w_right, w_right_gate], axis=1)
    projected = jnp.einsum(
        "rcd,dh->hrc", normalized_input, stacked, preferred_element_type=jnp.float32
    )
    q_left, p_left, q_right, p_right = jnp.split(projected, 4, axis=0)
    s_left = jax.nn.sigmoid(p_left)
    s_right = jax.nn.sigmoid(p_right)
    left = (s_left * q_left).astype(jnp.bfloat16)
    right = (s_right * q_right).astype(jnp.bfloat16)
    g_chan, left_chan, right_chan = (
        lax.all_to_all(cotangent, "col", split_axis=0, concat_axis=2, tiled=True),
        lax.all_to_all(left, "col", split_axis=0, concat_axis=2, tiled=True),
        lax.all_to_all(right, "col", split_axis=0, concat_axis=2, tiled=True),
    )
    residues = g_chan.shape[2]
    col_block = g_chan
    d_left = jnp.einsum(
        "hij,hjk->hik",
        col_block,
        lax.all_gather(right_chan, "row", axis=1, tiled=True),
        preferred_element_type=jnp.float32,
    )
    col_block = g_chan
    summed = lax.psum_scatter(
        jnp.einsum("hij,hik->jhk", col_block, left_chan, preferred_element_type=jnp.float32),
        "row",
        scatter_dimension=0,
        tiled=True,
    )
    d_right = jnp.transpose(summed, (1, 0, 2))
    d_left_tile, d_right_tile = (
        lax.all_to_all(d_left.astype(jnp.bfloat16), "col", split_axis=2, concat_axis=0, tiled=True),
        lax.all_to_all(
            d_right.astype(jnp.bfloat16), "col", split_axis=2, concat_axis=0, tiled=True
        ),
    )
    grad_l = d_left_tile.astype(jnp.float32)
    grad_r = d_right_tile.astype(jnp.float32)
    e_left = grad_l * s_left
    f_left = grad_l * q_left * s_left * (1.0 - s_left)
    e_right = grad_r * s_right
    f_right = grad_r * q_right * s_right * (1.0 - s_right)
    grads = jnp.concatenate([e_left, f_left, e_right, f_right], axis=0).astype(jnp.bfloat16)
    local_weights = jnp.einsum(
        "rcd,hrc->dh", normalized_input, grads, preferred_element_type=jnp.float32
    )
    total_weights = lax.psum(local_weights, ("row", "col")) / residues
    normalized_gradient = jnp.einsum(
        "hrc,dh->rcd", grads, stacked, preferred_element_type=jnp.float32
    )
    gradient_mean = jnp.mean(normalized_gradient, axis=-1, keepdims=True)
    gradient_input_mean = jnp.mean(normalized_gradient * standardized_input, axis=-1, keepdims=True)
    pair_gradient = (
        (normalized_gradient - gradient_mean - standardized_input * gradient_input_mean)
        * inverse_scale
    ).astype(jnp.bfloat16)
    pieces_w = jnp.split(total_weights, 4, axis=1)
    return (pair_gradient, pieces_w[0], pieces_w[1], pieces_w[2], pieces_w[3])


def solution(mesh):
    in_specs = (P("row", "col", None), P(None, "row", "col"), P(), P(), P(), P())
    out_specs = (P("row", "col", None), P(), P(), P(), P())
    return jax.shard_map(shards, mesh=mesh, in_specs=in_specs, out_specs=out_specs, check_vma=False)
```

profile of v0, /device:TPU:2, one launch (start us, length us, event | category | flops | bytes accessed | tf_op | source)
XLA Modules:
  0.0 579.7 jit_solution(9537658770375944991)
XLA Ops:
  7.2 1.2 convert_reduce_fusion
  8.4 1.3 fusion.10
  9.8 0.8 copy.87
  10.6 0.8 copy.88
  11.4 0.8 copy.89
  12.3 0.8 copy.90
  13.1 1.4 fusion.18
  14.6 0.2 multiply_convert_fusion.5
  14.8 0.3 copy.91
  15.1 0.2 reshape.47
  15.3 21.4 %all_to_all.72 = bf16[8,2,4096]{2,1,0:T(2,128)(2,1)S(1)} all-to-all(bf16[8,2,4096]{2,1,0:T(2,128)(2,1)S(1)} %reshape.47), channel_id=1, replica_groups=mesh['row'=32,'col'=8] {'col'}, dimensions={0} | all-to-all | bytes 262144 | tf_op jit(solution)/shard_map/all_to_all | solution.py:27
  37.1 0.9 all_to_all.56
  38.0 0.2 reshape.45
  38.3 13.0 %all_to_all.73 = bf16[8,2,4096]{2,1,0:T(2,128)(2,1)S(1)} all-to-all(bf16[8,2,4096]{2,1,0:T(2,128)(2,1)S(1)} %reshape.45), channel_id=1, replica_groups=mesh['row'=32,'col'=8] {'col'}, dimensions={0} | all-to-all | bytes 262144 | tf_op jit(solution)/shard_map/all_to_all | solution.py:25
  51.7 0.2 all_to_all.60
  51.9 43.9 %all-gather.2.cloned.1.call-done = bf16[8,512,512]{2,1,0:T(8,128)(2,1)} async-done(((bf16[8,16,512]{2,1,0:T(8,128)(2,1)}), bf16[8,512,512]{2,1,0:T(8,128)(2,1)}) %all-gather.2.cloned.1.call-update) | async-done | bytes 4194320 | tf_op jit(solution)/shard_map/all_gather | solution.py:34
  95.9 2.8 fusion
  98.7 0.8 copy.94
  99.5 1.1 reshape.49
  100.5 18.0 %all_to_all.74 = bf16[8,2,4096]{2,1,0:T(2,128)(2,1)S(1)} all-to-all(bf16[8,2,4096]{2,1,0:T(2,128)(2,1)S(1)} %reshape.49), channel_id=1, replica_groups=mesh['row'=32,'col'=8] {'col'}, dimensions={0} | all-to-all | bytes 262144 | tf_op jit(solution)/shard_map/all_to_all | solution.py:46
  118.6 0.7 reshape.50
  119.3 0.7 copy.95
  120.2 0.3 copy.97
  120.5 0.4 multiply_convert_fusion.4
  120.9 0.3 copy.99
  121.2 0.2 reshape.51
  121.4 13.0 %all_to_all.75 = bf16[8,2,4096]{2,1,0:T(2,128)(2,1)S(1)} all-to-all(bf16[8,2,4096]{2,1,0:T(2,128)(2,1)S(1)} %reshape.51), channel_id=1, replica_groups=mesh['row'=32,'col'=8] {'col'}, dimensions={0} | all-to-all | bytes 262144 | tf_op jit(solution)/shard_map/all_to_all | solution.py:26
  134.8 0.2 all_to_all.65
  135.1 4.5 convolution_bitcast_fusion
  139.6 10.4 %copy.101 = f32[512,8,512]{2,1,0:T(8,128)} copy(f32[512,8,512]{0,2,1:T(8,128)} %convolution_bitcast_fusion) | data formatting | bytes 16777216 | tf_op jit(solution)/shard_map/hij,hik->jhk/transpose | solution.py:39
  150.1 150.5 %reduce-scatter.2.cloned.1.call-done = f32[16,8,512]{2,1,0:T(8,128)} async-done(((f32[512,8,512]{2,1,0:T(8,128)}), f32[16,8,512]{2,1,0:T(8,128)}) %reduce-scatter.2.cloned.1.call-update) | async-done | bytes 262160 | tf_op jit(solution)/shard_map/reduce_scatter | solution.py:38
  300.5 1.0 convert_bitcast_fusion
  301.5 0.8 copy.102
  302.3 1.1 reshape.53
  303.4 16.3 %all_to_all.76 = bf16[8,2,4096]{2,1,0:T(2,128)(2,1)S(1)} all-to-all(bf16[8,2,4096]{2,1,0:T(2,128)(2,1)S(1)} %reshape.53), channel_id=1, replica_groups=mesh['row'=32,'col'=8] {'col'}, dimensions={0} | all-to-all | bytes 262144 | tf_op jit(solution)/shard_map/all_to_all | solution.py:47
  319.7 0.7 reshape.54
  320.4 0.7 copy.103
  321.4 0.3 copy.105
  321.6 0.3 multiply_convert_fusion.1
  322.0 1.5 convolution_bitcast_fusion.1
  323.5 1.0 fusion.21
  324.5 1.3 fusion.9
  325.9 243.5 %all-reduce.2.cloned.1.call-done = f32[128,256]{1,0:T(8,128)} async-done(((f32[128,256]{1,0:T(8,128)}), f32[128,256]{1,0:T(8,128)}) %all-reduce.2.cloned.1.call-update) | async-done | bytes 131088 | tf_op jit(solution)/shard_map/psum | solution.py:61
  569.4 0.9 broadcast_multiply_fusion
  570.4 0.7 copy.110
  571.1 0.7 copy.109
  571.8 0.7 copy.108
  572.5 0.7 copy.107
  (24 shorter events, 1.9 us)
Async XLA Ops:
  7.2 30.9 %copy-start.1 = (bf16[64,16,64]{2,1,0:T(8,128)(2,1)S(1)}, bf16[64,16,64]{2,1,0:T(8,128)(2,1)}, u32[]{:S(2)}) copy-start(bf16[64,16,64]{2,1,0:T(8,128)(2,1)} %param.7) | copy-start | bytes 393220
  7.2 88.7 %all-gather.2.cloned.1.call-start = ((), (), s32[]{:S(2)}) async-start(), calls=%async_computation.6 | async-start | bytes 4325376 | tf_op jit(solution)/shard_map/all_gather | solution.py:34
  38.0 262.5 %reduce-scatter.2.cloned.1.call-start = ((), (), s32[]{:S(2)}) async-start(), calls=%async_computation.7 | async-start | bytes 8650752 | tf_op jit(solution)/shard_map/reduce_scatter | solution.py:38
  150.0 419.4 %all-reduce.2.cloned.1.call-start = ((), (), s32[]{:S(2)}) async-start(), calls=%async_computation.8 | async-start | bytes 262144 | tf_op jit(solution)/shard_map/psum | solution.py:61
  302.3 19.7 %copy-start = (bf16[16,64,128]{2,1,0:T(8,128)(2,1)S(1)}, bf16[16,64,128]{2,1,0:T(8,128)(2,1)}, u32[]{:S(2)}) copy-start(bf16[16,64,128]{2,1,0:T(8,128)(2,1)} %param.6) | copy-start | bytes 786436
Sparse Core Ops, SparseCore 0:
  38.1 57.7 all-gather.1
  150.1 150.3 reduce-scatter.1
  324.7 244.7 all-reduce.1
where the time goes:
time: 581 us; the launch traced here: 580 us
  waiting for transfers between devices  438 us (75%)
  blocking collectives  81.8 us (14%)
  local copies, waits for them, and re-layouts  27.9 us (5%)
  between operations  14 us (2%)
  matrix products  11.3 us (2%)
  other arithmetic  6.66 us (1%)
    psum x1, waiting for transfers between devices, shards(): total_weights = lax.psum(local_weights, ('row', 'col')) / residues  244 us
    reduce_scatter x1, waiting for transfers between devices, shards(): lax.psum_scatter(jnp.einsum('hij,hik->jhk', col_block, left_chan, preferr...  150 us
    all_gather x1, waiting for transfers between devices, shards(): lax.all_gather(right_chan, 'row', axis=1, tiled=True)  43.9 us
    all_to_all x1, blocking collectives, shards(): lax.all_to_all(right, 'col', split_axis=0, concat_axis=2, tiled=True)  21.4 us
    all_to_all x1, blocking collectives, shards(): lax.all_to_all(d_left.astype(jnp.bfloat16), 'col', split_axis=2, concat_a...  18 us
    all_to_all x1, blocking collectives, shards(): lax.all_to_all(d_right.astype(jnp.bfloat16), 'col', split_axis=2, concat_...  16.3 us
    all_to_all x1, blocking collectives, shards(): lax.all_to_all(left, 'col', split_axis=0, concat_axis=2, tiled=True)  13 us
    all_to_all x1, blocking collectives, shards(): lax.all_to_all(cotangent, 'col', split_axis=0, concat_axis=2, tiled=True)  13 us
  transfers between devices with their start and end apart: 3, of which 3 were waited for; matrix products, arithmetic and copies ran while one was open for 0% of the time, Pallas kernels for 0%

commit v1 on v0

--- a/solution.py
+++ b/solution.py
@@ -2,6 +2,12 @@
 import jax.numpy as jnp
 from jax import lax
 from jax.sharding import PartitionSpec as P
+
+
+def summed_here(x, name):
+    parts = lax.all_gather(x, name, axis=0, tiled=False)
+    total = parts.sum(axis=0)
+    return total
 
 
 def shards(pair, cotangent, w_left, w_left_gate, w_right, w_right_gate):
@@ -58,7 +64,7 @@
     local_weights = jnp.einsum(
         "rcd,hrc->dh", normalized_input, grads, preferred_element_type=jnp.float32
     )
-    total_weights = lax.psum(local_weights, ("row", "col")) / residues
+    total_weights = summed_here(local_weights, ("row", "col")) / residues
     normalized_gradient = jnp.einsum(
         "hrc,dh->rcd", grads, stacked, preferred_element_type=jnp.float32
     )

time: 581 us -> 1100 us (1.89)
  waiting for transfers between devices: 438 us -> 940 us
  other arithmetic: 6.66 us -> 17.9 us
    all_gather x0 -> x1, waiting for transfers between devices: none -> 746 us  [summed_here(): parts = lax.all_gather(x, name, axis=0, tiled=False)]
    psum x1 -> x0, waiting for transfers between devices: 244 us -> none  [shards(): total_weights = lax.psum(local_weights, ('row', 'col')) / residues]
    reduce_sum x0 -> x1, other arithmetic: none -> 12.2 us  [summed_here(): total = parts.sum(axis=0)]
where the time goes in v1:
time: 1100 us; the launch traced here: 1090 us
  waiting for transfers between devices  940 us (85%)
  blocking collectives  81.5 us (7%)
  local copies, waits for them, and re-layouts  28.8 us (3%)
  other arithmetic  17.9 us (2%)
  between operations  14 us (1%)
  matrix products  11.2 us (1%)
    all_gather x1, waiting for transfers between devices, summed_here(): parts = lax.all_gather(x, name, axis=0, tiled=False)  746 us
    reduce_scatter x1, waiting for transfers between devices, shards(): lax.psum_scatter(jnp.einsum('hij,hik->jhk', col_block, left_chan, preferr...  150 us
    all_gather x1, waiting for transfers between devices, shards(): lax.all_gather(right_chan, 'row', axis=1, tiled=True)  43.7 us
  transfers between devices with their start and end apart: 3, of which 3 were waited for; matrix products, arithmetic and copies ran while one was open for 0% of the time, Pallas kernels for 0%

profile of v1, /device:TPU:2, one launch (start us, length us, event | category | flops | bytes accessed | tf_op | source)
XLA Modules:
  0.0 1093.5 jit_solution(17165267375763809610)
XLA Ops:
  7.2 1.2 convert_reduce_fusion
  8.4 1.3 fusion.10
  9.7 0.8 copy.79
  10.6 0.8 copy.80
  11.4 0.8 copy.81
  12.2 0.8 copy.82
  13.1 1.4 fusion.18
  14.5 0.2 multiply_convert_fusion.5
  14.8 0.3 copy.83
  15.0 0.2 reshape.48
  15.3 21.4 %all_to_all.72 = bf16[8,2,4096]{2,1,0:T(2,128)(2,1)S(1)} all-to-all(bf16[8,2,4096]{2,1,0:T(2,128)(2,1)S(1)} %reshape.48), channel_id=1, replica_groups=mesh['row'=32,'col'=8] {'col'}, dimensions={0} | all-to-all | bytes 262144 | tf_op jit(solution)/shard_map/all_to_all | solution.py:33
  36.6 0.2 reshape.49
  37.0 0.9 all_to_all.56
  38.0 1.2 reshape.46
  39.2 13.0 %all_to_all.73 = bf16[8,2,4096]{2,1,0:T(2,128)(2,1)S(1)} all-to-all(bf16[8,2,4096]{2,1,0:T(2,128)(2,1)S(1)} %reshape.46), channel_id=1, replica_groups=mesh['row'=32,'col'=8] {'col'}, dimensions={0} | all-to-all | bytes 262144 | tf_op jit(solution)/shard_map/all_to_all | solution.py:31
  52.2 0.2 reshape.47
  52.8 43.7 %all-gather.4.cloned.1.call-done = bf16[8,512,512]{2,1,0:T(8,128)(2,1)} async-done(((bf16[8,16,512]{2,1,0:T(8,128)(2,1)}), bf16[8,512,512]{2,1,0:T(8,128)(2,1)}) %all-gather.4.cloned.1.call-update) | async-done | bytes 4194320 | tf_op jit(solution)/shard_map/all_gather | solution.py:40
  96.5 2.8 fusion
  99.4 0.8 copy.86
  100.2 1.1 reshape.50
  101.2 17.4 %all_to_all.74 = bf16[8,2,4096]{2,1,0:T(2,128)(2,1)S(1)} all-to-all(bf16[8,2,4096]{2,1,0:T(2,128)(2,1)S(1)} %reshape.50), channel_id=1, replica_groups=mesh['row'=32,'col'=8] {'col'}, dimensions={0} | all-to-all | bytes 262144 | tf_op jit(solution)/shard_map/all_to_all | solution.py:52
  118.6 0.7 reshape.51
  119.3 0.7 copy.87
  120.3 0.3 copy.89
  120.5 0.4 multiply_convert_fusion.4
  120.9 0.3 copy.91
  121.2 0.2 reshape.52
  121.4 13.0 %all_to_all.75 = bf16[8,2,4096]{2,1,0:T(2,128)(2,1)S(1)} all-to-all(bf16[8,2,4096]{2,1,0:T(2,128)(2,1)S(1)} %reshape.52), channel_id=1, replica_groups=mesh['row'=32,'col'=8] {'col'}, dimensions={0} | all-to-all | bytes 262144 | tf_op jit(solution)/shard_map/all_to_all | solution.py:32
  135.1 4.5 convolution_bitcast_fusion
  139.6 10.4 copy.93
  150.1 150.4 %reduce-scatter.2.cloned.1.call-done = f32[16,8,512]{2,1,0:T(8,128)} async-done(((f32[512,8,512]{2,1,0:T(8,128)}), f32[16,8,512]{2,1,0:T(8,128)}) %reduce-scatter.2.cloned.1.call-update) | async-done | bytes 262160 | tf_op jit(solution)/shard_map/reduce_scatter | solution.py:44
  300.5 1.0 convert_bitcast_fusion
  301.5 0.8 copy.94
  302.3 1.1 reshape.54
  303.4 16.7 %all_to_all.76 = bf16[8,2,4096]{2,1,0:T(2,128)(2,1)S(1)} all-to-all(bf16[8,2,4096]{2,1,0:T(2,128)(2,1)S(1)} %reshape.54), channel_id=1, replica_groups=mesh['row'=32,'col'=8] {'col'}, dimensions={0} | all-to-all | bytes 262144 | tf_op jit(solution)/shard_map/all_to_all | solution.py:53
  320.0 0.7 reshape.55
  320.7 0.7 copy.95
  321.7 0.3 copy.97
  322.0 0.3 multiply_convert_fusion.1
  322.3 1.5 convolution_bitcast_fusion.1
  323.8 1.0 fusion.21
  324.8 1.3 fusion.9
  326.1 745.8 %all-gather.6.cloned.1.call-done = f32[32768,256]{1,0:T(8,128)} async-done(((f32[128,256]{1,0:T(8,128)}), f32[32768,256]{1,0:T(8,128)}) %all-gather.6.cloned.1.call-update) | async-done | bytes 33554448 | tf_op jit(solution)/shard_map/all_gather | solution.py:8
  1071.9 12.2 %reduce_sum.49 = f32[128,256]{1,0:T(8,128)S(1)} reduce(f32[256,128,256]{2,1,0:T(8,128)} %bitcast.43, f32[]{:T(128)} %constant.12.clone.1), dimensions={0}, to_apply=%region_5.0 | reduce | flops 8355840 | bytes 33685508 | tf_op jit(solution)/shard_map/reduce_sum | solution.py:9
  1084.2 0.7 copy.102
  1084.9 0.7 copy.101
  1085.6 0.7 copy.100
  1086.3 0.7 copy.99
  (23 shorter events, 1.9 us)
Async XLA Ops:
  7.2 89.4 %all-gather.4.cloned.1.call-start = ((), (), s32[]{:S(2)}) async-start(), calls=%async_computation.6 | async-start | bytes 4325376 | tf_op jit(solution)/shard_map/all_gather | solution.py:40
  37.9 262.6 %reduce-scatter.2.cloned.1.call-start = ((), (), s32[]{:S(2)}) async-start(), calls=%async_computation.7 | async-start | bytes 8650752 | tf_op jit(solution)/shard_map/reduce_scatter | solution.py:44
  150.0 172.3 %copy-start = (bf16[16,64,128]{2,1,0:T(8,128)(2,1)S(1)}, bf16[16,64,128]{2,1,0:T(8,128)(2,1)}, u32[]{:S(2)}) copy-start(bf16[16,64,128]{2,1,0:T(8,128)(2,1)} %param.6) | copy-start | bytes 786436
  150.0 921.8 %all-gather.6.cloned.1.call-start = ((), (), s32[]{:S(2)}) async-start(), calls=%async_computation.8 | async-start | bytes 33685504 | tf_op jit(solution)/shard_map/all_gather | solution.py:8
Sparse Core Ops, SparseCore 0:
  38.1 58.4 all-gather.3
  150.2 150.3 reduce-scatter.1
  323.9 747.8 all-gather.5
